TPU v7x, 32 devices: a whole 2x2x4 slice. The times are simulated.
32 devices in a mesh: seq: 8 (over z, x), tp: 4 (over y, core).
Axes of the slice: x: 2, y: 2, z: 4, core: 2. Of those that a mesh axis runs over, the one named last changes fastest.
Arguments:
- byte_states: bfloat16 [4096, 1024], P('seq'), may hold values from -6 to 6
- flags: int32 [4096], P('seq'), may hold values from 0 to 1, as said below
- stretch_owner: int32 [1024, 1], P('seq'), may hold values from 0 to 7; in each aligned block of 128 rows (0 to 127, 128 to 255, ...) at most 32 rows name the same one
- log_decay: float32 [4096, 16], P('seq', 'tp'), may hold values from -2 to 0, as said below
- w_x: bfloat16 [1024, 2048], P(None, 'tp'), may hold values from -0.1875 to 0.1875
- w_z: bfloat16 [1024, 2048], P(None, 'tp'), may hold values from -0.1875 to 0.1875
- w_bc: bfloat16 [1024, 256], replicated, may hold values from -0.1875 to 0.1875
- w_out: bfloat16 [2048, 1024], P('tp'), may hold values from -0.125 to 0.125
- pad_vector: bfloat16 [512], replicated, may hold values from -5 to 5
- w_q: bfloat16 [1536, 1536], P(None, 'tp'), may hold values from -8 to 8
- w_k: bfloat16 [1536, 1536], P(None, 'tp'), may hold values from -8 to 8
- w_v: bfloat16 [1536, 1536], P(None, 'tp'), may hold values from -0.15625 to 0.15625
- w_o: bfloat16 [1536, 1536], P('tp'), may hold values from -0.15625 to 0.15625
Outputs:
- enc_out: bfloat16 [4096, 1024], P('seq', 'tp')
- main_out: bfloat16 [2048, 1536], P('seq')
Inputs may be any that keep to these rules, and one draw needn't show every extreme that they name: `flags`: exactly 128 ones among each aligned block of 512 bytes. `stretch_owner`: in each aligned block of 128 stretches no owner is named more than 32 times. `log_decay`: negative.
All inputs are finite; a program needn't handle non-finite values.
Results may differ from a plain program's by a relative error of at most 0.015.
Values may be sent and summed in bfloat16 or wider, within the bound.
A program may use at most 128 MiB of HBM per device.

v0:
```python
import math
import jax
import jax.numpy as jnp
from jax import lax
from jax.sharding import PartitionSpec as P

HD = 128
BLOCK = 256
eps = 1e-05
highest = lax.Precision.HIGHEST
far_query = 536870912
far_key = 1073741824


def carried_in(shard, axis, combine, identity):
    peers, index = (lax.axis_size(axis), lax.axis_index(axis))
    everything = jax.tree.map(
        lambda part, kind: lax.all_gather(part.astype(kind), axis),
        shard,
        (jnp.bfloat16, jnp.bfloat16),
    )
    start = jax.tree.map(
        lambda part, zero: jnp.broadcast_to(jnp.asarray(zero, part.dtype), part.shape),
        shard,
        identity,
    )

    def carried_step(k, before):
        reached = k < index
        new = combine(
            before, jax.tree.map(lambda part, own: part[k].astype(own.dtype), everything, shard)
        )
        return jax.tree.map(lambda a, b: jnp.where(reached, a, b), new, before)

    return lax.fori_loop(0, peers, carried_step, start)


def shortened(shard):

    def short(part):
        return part.astype(jnp.bfloat16) if part.dtype == jnp.float32 else part

    return jax.tree.map(short, shard)


def rms_rows(values):
    wide = values.astype(jnp.float32)
    return wide * lax.rsqrt(jnp.mean(wide * wide, axis=-1, keepdims=True) + eps)


def ssd_blocks(xh, bmat, cmat, decay, start_state):
    rows, heads, width_p = xh.shape
    nblk = rows // BLOCK

    def advance(state, block):
        x_blk, b_blk, c_blk, a_blk = block
        cum = jnp.cumsum(a_blk, axis=0)
        later = lax.broadcasted_iota(jnp.int32, (BLOCK, BLOCK), 0)
        earlier = lax.broadcasted_iota(jnp.int32, (BLOCK, BLOCK), 1)
        causal = (later >= earlier)[:, :, None]
        spans = jnp.where(causal, cum[:, None, :] - cum[None, :, :], -1e30)
        intersection = jnp.dot(c_blk, b_blk.T, preferred_element_type=jnp.float32)
        mixing = intersection[:, :, None] * jnp.exp(spans)
        x_wide = x_blk.astype(jnp.float32)
        inside = jnp.einsum("tsh,shp->thp", mixing, x_wide, precision=highest)
        carried = (
            jnp.einsum("tn,hnp->thp", c_blk.astype(jnp.float32), state, precision=highest)
            * jnp.exp(cum)[:, :, None]
        )
        tail = jnp.exp(cum[-1][None, :] - cum)
        fresh = jnp.einsum(
            "sh,sn,shp->hnp", tail, b_blk.astype(jnp.float32), x_wide, precision=highest
        )
        new_state = state * jnp.exp(cum[-1])[:, None, None] + fresh
        return (new_state, inside + carried)

    blocks = (
        xh.reshape(nblk, BLOCK, heads, width_p),
        bmat.reshape(nblk, BLOCK, -1),
        cmat.reshape(nblk, BLOCK, -1),
        decay.reshape(nblk, BLOCK, heads),
    )
    final, outs = lax.scan(advance, start_state, blocks)
    return (outs.reshape(rows, heads, width_p), final)


def link_states(earlier, later):
    return (earlier[0] + later[0], earlier[1] * jnp.exp(later[0])[..., None, None] + later[1])


def attend_block(carry, queries, query_pos, key_blk, value_blk, key_pos, scale):
    best, total, accum = carry
    scores = (
        jnp.einsum("qhd,khd->hqk", queries, key_blk, preferred_element_type=jnp.float32) * scale
    )
    allowed = key_pos[None, None, :] <= query_pos[None, :, None]
    scores = jnp.where(allowed, scores, -1e30)
    new_best = jnp.maximum(best, jnp.max(scores, axis=2))
    shrink = jnp.exp(best - new_best)
    expo = jnp.where(allowed, jnp.exp(scores - new_best[:, :, None]), 0.0)
    total = total * shrink + jnp.sum(expo, axis=2)
    accum = accum * jnp.transpose(shrink)[:, :, None] + jnp.einsum(
        "hqk,khd->qhd", expo.astype(jnp.bfloat16), value_blk, preferred_element_type=jnp.float32
    )
    return (new_best, total, accum)


def on_device(
    byte_states,
    flags,
    stretch_owner,
    log_decay,
    w_x,
    w_z,
    w_bc,
    w_out,
    pad_vector,
    w_q,
    w_k,
    w_v,
    w_o,
):
    rows, width = byte_states.shape
    heads_here = log_decay.shape[1]
    head_p = w_x.shape[1] // heads_here
    state_n = w_bc.shape[1] // 2
    ranks = lax.axis_size("seq")
    split_tp = lax.axis_size("tp")
    normed = rms_rows(byte_states).astype(jnp.bfloat16)
    xs = jnp.dot(normed, w_x, preferred_element_type=jnp.float32).astype(jnp.bfloat16)
    zgate = jnp.dot(normed, w_z, preferred_element_type=jnp.float32)
    projected = jnp.dot(normed, w_bc, preferred_element_type=jnp.float32).astype(jnp.bfloat16)
    bmat = projected[:, :state_n]
    cmat = projected[:, state_n:]
    start_state = jnp.zeros((heads_here, state_n, head_p), jnp.float32)
    local_mixed, final = ssd_blocks(
        xs.reshape(rows, heads_here, head_p), bmat, cmat, log_decay, start_state
    )
    running = jnp.cumsum(log_decay, axis=0)
    identity = (jnp.zeros((heads_here,), jnp.float32), jnp.zeros_like(final))
    carried = carried_in((running[-1], final), "seq", link_states, identity)
    incoming = carried[1]
    mixed = (
        local_mixed
        + jnp.einsum("tn,hnp->thp", cmat.astype(jnp.float32), incoming, precision=highest)
        * jnp.exp(running)[:, :, None]
    )
    gated = mixed * jax.nn.silu(zgate).reshape(rows, heads_here, head_p)
    scaled = gated * lax.rsqrt(jnp.mean(gated * gated, axis=2, keepdims=True) + eps)
    scaled = scaled.reshape(rows, heads_here * head_p).astype(jnp.bfloat16)
    partial_enc = jnp.dot(scaled, w_out, preferred_element_type=jnp.float32)
    quarter = width // split_tp
    column_start = lax.axis_index("tp") * quarter
    stretches_here = stretch_owner.shape[0]
    flag_rank = jnp.cumsum(flags) - 1
    stretch_ids = lax.broadcasted_iota(jnp.int32, (stretches_here, rows), 0)
    picker = ((flag_rank[None, :] == stretch_ids) & (flags[None, :] == 1)).astype(jnp.bfloat16)
    summed = lax.psum(partial_enc.astype(jnp.bfloat16), "tp").astype(jnp.float32)
    encoded = (byte_states.astype(jnp.float32) + summed).astype(jnp.bfloat16)
    enc_out = lax.dynamic_slice_in_dim(encoded, column_start, quarter, 1)
    stretch_rows = jnp.dot(picker, encoded, preferred_element_type=jnp.float32).astype(jnp.bfloat16)
    cap = max(2, 2 * stretches_here // ranks)
    slots = ranks * cap
    owners = stretch_owner[:, 0]
    owner_hot = (
        owners[:, None] == lax.broadcasted_iota(jnp.int32, (stretches_here, ranks), 1)
    ).astype(jnp.int32)
    before = jnp.cumsum(owner_hot, axis=0) - owner_hot
    order = jnp.sum(before * owner_hot, axis=1)
    slot = owners * cap + order
    slot_ids = lax.broadcasted_iota(jnp.int32, (slots, stretches_here), 0)
    placed = slot_ids == slot[None, :]
    anchor = lax.axis_index("seq") * stretches_here + lax.broadcasted_iota(
        jnp.int32, (stretches_here,), 0
    )
    send_pos = jnp.where(
        jnp.any(placed, axis=1), jnp.sum(jnp.where(placed, anchor[None, :], 0), axis=1), -1
    )
    send_rows = jnp.dot(
        placed.astype(jnp.bfloat16), stretch_rows, preferred_element_type=jnp.float32
    ).astype(jnp.bfloat16)
    got_rows, got_pos = (
        lax.all_to_all(
            send_rows.reshape(ranks, cap, width), "seq", split_axis=0, concat_axis=0, tiled=True
        ),
        lax.all_to_all(
            send_pos.reshape(ranks, cap), "seq", split_axis=0, concat_axis=0, tiled=True
        ),
    )
    got_rows = got_rows.reshape(slots, width)
    got_pos = got_pos.reshape(slots)
    valid = got_pos >= 0
    padding = jnp.where(valid[:, None], pad_vector[None, :], jnp.zeros((), jnp.bfloat16))
    stream = jnp.concatenate([got_rows, padding], axis=1)
    stream_norm = rms_rows(stream).astype(jnp.bfloat16)
    heads_main = w_q.shape[1] // HD
    scale = 1.0 / math.sqrt(HD)
    queries = (
        jnp.dot(stream_norm, w_q, preferred_element_type=jnp.float32)
        .astype(jnp.bfloat16)
        .reshape(slots, heads_main, HD)
    )
    query_pos = jnp.where(valid, got_pos, far_query)
    start_carry = (
        jnp.full((heads_main, slots), -1e30, jnp.float32),
        jnp.zeros((heads_main, slots), jnp.float32),
        jnp.zeros((slots, heads_main, HD), jnp.float32),
    )
    keys_here = (
        jnp.dot(stream_norm, w_k, preferred_element_type=jnp.float32)
        .astype(jnp.bfloat16)
        .reshape(slots, heads_main, HD)
    )
    values_here = (
        jnp.dot(stream_norm, w_v, preferred_element_type=jnp.float32)
        .astype(jnp.bfloat16)
        .reshape(slots, heads_main, HD)
    )
    key_pos_here = jnp.where(valid, got_pos, far_key)
    key_rows = lax.all_gather(keys_here, "seq", axis=0, tiled=True)
    count = key_rows.shape[0]
    size = math.gcd(count, 512)
    nblk = count // size

    def fold_step(state, block):
        return (attend_block(state, queries, query_pos, block[0], block[1], block[2], scale), None)

    blocks = (
        key_rows.reshape(nblk, size, heads_main, HD),
        lax.all_gather(values_here, "seq", axis=0, tiled=True).reshape(nblk, size, heads_main, HD),
        lax.all_gather(shortened(key_pos_here), "seq", axis=0, tiled=True).reshape(nblk, size),
    )
    best, total, accum = lax.scan(fold_step, start_carry, blocks)[0]
    attended = (
        (accum / jnp.transpose(total)[:, :, None])
        .astype(jnp.bfloat16)
        .reshape(slots, heads_main * HD)
    )
    summed_main = lax.psum(
        jnp.dot(attended, w_o, preferred_element_type=jnp.float32).astype(jnp.bfloat16), "tp"
    ).astype(jnp.float32)
    main_out = jnp.where(valid[:, None], stream.astype(jnp.float32) + summed_main, 0.0).astype(
        jnp.bfloat16
    )
    return (enc_out, main_out)


def solution(mesh):
    placed = (
        P("seq", None),
        P("seq"),
        P("seq", None),
        P("seq", "tp"),
        P(None, "tp"),
        P(None, "tp"),
        P(),
        P("tp", None),
        P(),
        P(None, "tp"),
        P(None, "tp"),
        P(None, "tp"),
        P("tp", None),
    )
    return jax.shard_map(
        on_device,
        mesh=mesh,
        in_specs=placed,
        out_specs=(P("seq", "tp"), P("seq", None)),
        check_vma=False,
    )
```

profile of v0, /device:TPU:0, one launch (start us, length us, event | category | flops | bytes accessed | tf_op | source)
XLA Modules:
  0.0 318.6 jit_solution(18168973310382984664)
XLA Ops:
  8.9 2.0 convolution_convert_fusion.4
  12.5 32.7 %while.42 = (s32[]{:T(128)}, f32[4,128,128]{2,1,0:T(8,128)S(1)}, f32[2,256,4,128]{1,0,3,2:T(2,128)}, f32[2,256,4]{1,2,0:T(4,128)S(1)}, bf16[2,256,128]{2,1,0:T(8...) while((s32[]{:T(128)}, f32[4,128,128]{2,1,0:T(8,128)S(1)}, ...), condition=%wide.region_4.5_spmd.clone, body=%wide.region_1.4_spmd.clone.sunk | while | flops 823755776 | bytes 7013988 | solution.py:83
  17.3 11.5 %dynamic_update_slice.6 = f32[2,256,4,128]{1,0,3,2:T(2,128)} dynamic-update-slice(f32[2,256,4,128]{1,0,3,2:T(2,128)} %get-tuple-element.594, f32[1,256,4,128]{1,0,3,2:T(1,128)S(1)} %copy.191, s32[]{:T(128)S(6)} %copy.196, s32[]{:T(128)} %constant.107.clone.1..sunk, s32[]{:T(128)} %constant.107.clone.1..sunk, s32[]{:T(128)} %constant.107.clone.1..sunk) | dynamic-update-slice | bytes 1048580 | tf_op jit(solution)/shard_map/while/body/jit(dynamic_update_index_in_dim)/dynamic_update_slice | solution.py:83
  33.7 11.5 %dynamic_update_slice.6 = f32[2,256,4,128]{1,0,3,2:T(2,128)} dynamic-update-slice(f32[2,256,4,128]{1,0,3,2:T(2,128)} %get-tuple-element.594, f32[1,256,4,128]{1,0,3,2:T(1,128)S(1)} %copy.191, s32[]{:T(128)S(6)} %copy.196, s32[]{:T(128)} %constant.107.clone.1..sunk, s32[]{:T(128)} %constant.107.clone.1..sunk, s32[]{:T(128)} %constant.107.clone.1..sunk) | dynamic-update-slice | bytes 1048580 | tf_op jit(solution)/shard_map/while/body/jit(dynamic_update_index_in_dim)/dynamic_update_slice | solution.py:83
  49.6 7.3 %all-to-all-start = ((s32[8,1,32]{2,1,0:T(1,128)}), s32[8,1,32]{2,1,0:T(1,128)}, u32[]{:S(2)}, u32[]{:S(2)}) async-start(s32[8,1,32]{2,1,0:T(1,128)} %select_n.72), calls=%async_computation | async-start | bytes 8192 | tf_op jit(solution)/shard_map/all_to_all | solution.py:186
  56.9 21.2 %all-gather.1 = bf16[8,1,4]{2,1,0:T(2,128)(2,1)} all-gather(bf16[1,1,4]{2,1,0:T(2,128)(2,1)S(1)} %slice_bitcast_fusion), channel_id=1, replica_groups=mesh['seq'=8,'tp'=4] {'seq'}, dimensions={0}, use_global_device_ids=true | all-gather | bytes 72 | tf_op jit(solution)/shard_map/all_gather | solution.py:18
  78.1 2.1 reshape.237
  83.3 3.2 %divide_multiply_fusion = f32[512,512]{0,1:T(8,128)} fusion(bf16[1024,512]{1,0:T(8,128)(2,1)} %param.24, bf16[512,1024]{1,0:T(8,128)(2,1)S(1)} %copy-done.5, f32[512]{0:T(512)} %copy-done.16), kind=kOutput, calls=%fused_computation.92 | convolution fusion | flops 539492352 | bytes 3147776 | tf_op jit(solution)/shard_map/dot_general | solution.py:131
  86.6 2.7 all-gather.11.cloned.1.call-done
  89.2 13.7 %while.43 = (s32[]{:T(128)}, f32[4,128,128]{2,1,0:T(8,128)S(1)}, s32[]{:T(128)}, bf16[8,4]{1,0:T(8,128)(2,1)}, bf16[8,4,128,128]{3,2,1,0:T(8,128)(2,1)}, /*index=5*/s32[]{:T(128)}, s32[]{:T(128)}) while((s32[]{:T(128)}, f32[4,128,128]{2,1,0:T(8,128)S(1)}, s32[]{:T(128)}, bf16[8,4]{1,0:T(8,128)(2,1)}, ...), condition=%wide.region_8.9_spmd.clone, body=%wide.region_7.8_spmd.clone.sunk | while | flops 327688 | bytes 655513 | solution.py:35
  109.1 34.9 %all-reduce.3.cloned.1.call-done = bf16[512,1024]{1,0:T(8,128)(2,1)} async-done(((bf16[512,1024]{1,0:T(8,128)(2,1)}), bf16[512,1024]{1,0:T(8,128)(2,1)}) %all-reduce.3.cloned.1.call-update) | async-done | bytes 1048592 | tf_op jit(solution)/shard_map/psum | solution.py:158
  147.0 5.5 %all-to-all-start.1 = ((bf16[8,32,1024]{2,1,0:T(8,128)(2,1)}), bf16[8,32,1024]{2,1,0:T(8,128)(2,1)S(1)}, u32[]{:S(2)}, u32[]{:S(2)}) async-start(bf16[8,32,1024]{2,1,0:T(8,128)(2,1)} %bitcast.182), calls=%async_computation.1 | async-start | bytes 1048576 | tf_op jit(solution)/shard_map/all_to_all | solution.py:183
  154.6 11.8 %all-to-all-done.1 = bf16[8,32,1024]{2,1,0:T(8,128)(2,1)S(1)} async-done(((bf16[8,32,1024]{2,1,0:T(8,128)(2,1)}), bf16[8,32,1024]{2,1,0:T(8,128)(2,1)S(1)}, u32[]{:S(2)}, u32[]{:S(2)}) %all-to-all-start.1) | async-done | bytes 524320 | tf_op jit(solution)/shard_map/all_to_all | solution.py:183
  166.7 1.9 convolution_convert_fusion.8
  169.7 1.9 convolution_convert_fusion.6
  172.5 18.7 %all-gather.2 = s32[8,1,256]{2,1,0:T(1,128)S(1)} all-gather(s32[1,1,256]{2,1,0:T(1,128)S(1)} %bitcast.201), channel_id=1, replica_groups=mesh['seq'=8,'tp'=4] {'seq'}, dimensions={0}, use_global_device_ids=true | all-gather | bytes 9216 | tf_op jit(solution)/shard_map/all_gather | solution.py:231
  191.2 1.9 convolution_convert_fusion.7
  193.4 19.5 %all-gather.7.cloned.1.call-done = bf16[2048,3,128]{0,2,1:T(8,128)(2,1)} async-done(((bf16[256,3,128]{0,2,1:T(8,128)(2,1)}), bf16[2048,3,128]{0,2,1:T(8,128)(2,1)}) %all-gather.7.cloned.1.call-update) | async-done | bytes 1572880 | tf_op jit(solution)/shard_map/all_gather | solution.py:220
  213.0 2.6 copy.141
  215.6 42.5 %all-gather.9.cloned.1.call-done = bf16[2048,3,128]{0,2,1:T(8,128)(2,1)} async-done(((bf16[256,3,128]{0,2,1:T(8,128)(2,1)}), bf16[2048,3,128]{0,2,1:T(8,128)(2,1)}) %all-gather.9.cloned.1.call-update) | async-done | bytes 1572880 | tf_op jit(solution)/shard_map/all_gather | solution.py:230
  258.1 2.6 copy.144
  260.7 14.2 %while.44 = (s32[]{:T(128)}, f32[3,256]{1,0:T(4,128)S(1)}, f32[3,256]{1,0:T(4,128)S(1)}, f32[256,3,128]{0,2,1:T(8,128)S(1)}, s32[4,512]{1,0:T(4,128)S(1)}, /*ind...) while((s32[]{:T(128)}, f32[3,256]{1,0:T(4,128)S(1)}, ...), condition=%wide.region_21.22_spmd.clone, body=%wide.region_18.21_spmd.clone.sunk | while | flops 205296128 | bytes 7068813 | solution.py:233
  278.1 31.7 %all-reduce.5.cloned.1.call-done = bf16[256,1536]{1,0:T(8,128)(2,1)} async-done(((bf16[256,1536]{1,0:T(8,128)(2,1)}), bf16[256,1536]{1,0:T(8,128)(2,1)}) %all-reduce.5.cloned.1.call-update) | async-done | bytes 786448 | tf_op jit(solution)/shard_map/psum | solution.py:239
  309.8 2.3 fusion.51
  (207 shorter events, 64.5 us)
Async XLA Ops:
  7.2 267.7 %copy-start = (bf16[384,1536]{1,0:T(8,128)(2,1)S(1)}, bf16[384,1536]{1,0:T(8,128)(2,1)}, u32[]{:S(2)}) copy-start(bf16[384,1536]{1,0:T(8,128)(2,1)} %param.31) | copy-start | bytes 3538948
  7.2 82.0 %all-gather.11.cloned.1.call-start = ((), (), s32[]{:S(2)}) async-start(), calls=%async_computation.6 | async-start | bytes 1179648 | tf_op jit(solution)/shard_map/all_gather | solution.py:18
  8.8 2.7 copy-start.4
  8.8 2.7 copy-start.18
  8.9 3.5 %copy-start.16 = (f32[512]{0:T(512)}, f32[512]{0:T(512)S(1)}, u32[]{:S(2)}) copy-start(f32[512]{0:T(512)S(1)} %add_rsqrt_fusion.1) | copy-start | bytes 6148
  12.5 35.3 %copy-start.13 = (s32[128,1]{0,1:T(1,128)S(1)}, s32[128,1]{0,1:T(1,128)}, u32[]{:S(2)}) copy-start(s32[128,1]{0,1:T(1,128)} %param.21) | copy-start | bytes 1540
  45.2 38.1 %copy-start.5 = (bf16[512,1024]{1,0:T(8,128)(2,1)S(1)}, bf16[512,1024]{1,0:T(8,128)(2,1)}, u32[]{:S(2)}) copy-start(bf16[512,1024]{1,0:T(8,128)(2,1)} %param.19) | copy-start | bytes 3145732
  49.6 97.4 %all-to-all-start = ((s32[8,1,32]{2,1,0:T(1,128)}), s32[8,1,32]{2,1,0:T(1,128)}, u32[]{:S(2)}, u32[]{:S(2)}) async-start(s32[8,1,32]{2,1,0:T(1,128)} %select_n.72), calls=%async_computation | async-start | bytes 8192 | tf_op jit(solution)/shard_map/all_to_all | solution.py:186
  56.9 87.2 %all-reduce.3.cloned.1.call-start = ((), (), s32[]{:S(2)}) async-start(), calls=%async_computation.2 | async-start | bytes 2097152 | tf_op jit(solution)/shard_map/psum | solution.py:158
  103.7 1.7 copy-start.8
  105.9 1.2 copy-start.19
  107.1 1.8 copy-start.11
  107.1 1.9 copy-start.12
  109.1 36.6 %copy-start.15 = (s32[128]{0:T(128)S(1)}, s32[128]{0:T(128)}, u32[]{:S(2)}) copy-start(s32[128]{0:T(128)} %copy-done.14) | copy-start | bytes 1540
  145.7 21.0 %copy-start.1 = (bf16[512,1024]{1,0:T(8,128)(2,1)}, bf16[512,1024]{1,0:T(8,128)(2,1)S(1)}, u32[]{:S(2)}) copy-start(bf16[512,1024]{1,0:T(8,128)(2,1)S(1)} %fusion.47) | copy-start | bytes 3145732
  145.7 8.8 %copy-start.17 = (bf16[512]{0:T(512)(128)(2,1)S(1)}, bf16[512]{0:T(512)(128)(2,1)}, u32[]{:S(2)}) copy-start(bf16[512]{0:T(512)(128)(2,1)} %param.27) | copy-start | bytes 3076
  147.0 19.5 %all-to-all-start.1 = ((bf16[8,32,1024]{2,1,0:T(8,128)(2,1)}), bf16[8,32,1024]{2,1,0:T(8,128)(2,1)S(1)}, u32[]{:S(2)}, u32[]{:S(2)}) async-start(bf16[8,32,1024]{2,1,0:T(8,128)(2,1)} %bitcast.182), calls=%async_computation.1 | async-start | bytes 1048576 | tf_op jit(solution)/shard_map/all_to_all | solution.py:183
  152.5 60.5 %all-gather.7.cloned.1.call-start = ((), (), s32[]{:S(2)}) async-start(), calls=%async_computation.3 | async-start | bytes 1769472 | tf_op jit(solution)/shard_map/all_gather | solution.py:220
  154.6 36.6 %copy-start.6 = (bf16[256,512]{1,0:T(8,128)(2,1)}, bf16[256,512]{1,0:T(8,128)(2,1)S(1)}, u32[]{:S(2)}) copy-start(bf16[256,512]{1,0:T(8,128)(2,1)S(1)} %broadcast_select_fusion) | copy-start | bytes 786436
  166.5 24.8 %copy-start.2 = (bf16[8,32,1024]{2,1,0:T(8,128)(2,1)}, bf16[8,32,1024]{2,1,0:T(8,128)(2,1)S(1)}, u32[]{:S(2)}) copy-start(bf16[8,32,1024]{2,1,0:T(8,128)(2,1)S(1)} %all-to-all-done.1) | copy-start | bytes 1572868
  169.5 88.6 %all-gather.9.cloned.1.call-start = ((), (), s32[]{:S(2)}) async-start(), calls=%async_computation.4 | async-start | bytes 1769472 | tf_op jit(solution)/shard_map/all_gather | solution.py:230
  172.4 137.4 %all-reduce.5.cloned.1.call-start = ((), (), s32[]{:S(2)}) async-start(), calls=%async_computation.5 | async-start | bytes 1572864 | tf_op jit(solution)/shard_map/psum | solution.py:239
  274.9 34.9 %copy-start.3 = (bf16[8,32,1024]{2,1,0:T(8,128)(2,1)S(1)}, bf16[8,32,1024]{2,1,0:T(8,128)(2,1)}, u32[]{:S(2)}) copy-start(bf16[8,32,1024]{2,1,0:T(8,128)(2,1)} %copy-done.2) | copy-start | bytes 1572868
  274.9 34.9 %copy-start.7 = (bf16[256,512]{1,0:T(8,128)(2,1)S(1)}, bf16[256,512]{1,0:T(8,128)(2,1)}, u32[]{:S(2)}) copy-start(bf16[256,512]{1,0:T(8,128)(2,1)} %copy-done.6) | copy-start | bytes 786436
  (3 other events, 2.1 us)
Sparse Core Ops, SparseCore 0:
  46.1 43.1 all-gather.10
  109.0 34.9 all-reduce.2
  169.6 43.3 all-gather.6
  215.4 42.5 all-gather.8
  276.5 33.2 all-reduce.4
where the time goes:
time: 321 us; the launch traced here: 319 us
  waiting for transfers between devices  143 us (45%)
  local copies, waits for them, and re-layouts  43 us (13%)
  blocking collectives  39.8 us (12%)
  matrix products  33.9 us (11%)
  other arithmetic  30.7 us (10%)
  between operations  14.2 us (4%)
  starting transfers between devices  13.2 us (4%)
    all_gather x1, waiting for transfers between devices, on_device(): lax.all_gather(values_here, 'seq', axis=0, tiled=True)  42.5 us
    psum x1, waiting for transfers between devices, on_device(): lax.psum(partial_enc.astype(jnp.bfloat16), 'tp').astype(jnp.float32)  34.9 us
    psum x1, waiting for transfers between devices, on_device(): lax.psum(jnp.dot(attended, w_o, preferred_element_type=jnp.float32).astyp...  31.7 us
    dynamic_update_slice x4, local copies, waits for them, and re-layouts, ssd_blocks(): final, outs = lax.scan(advance, start_state, blocks)  24.1 us
    all_gather x1, blocking collectives, carried_in(): lax.all_gather(part.astype(kind), axis)  21.2 us
    all_gather x1, waiting for transfers between devices, on_device(): key_rows = lax.all_gather(keys_here, 'seq', axis=0, tiled=True)  19.5 us
    all_gather x1, blocking collectives, on_device(): lax.all_gather(shortened(key_pos_here), 'seq', axis=0, tiled=True)  18.7 us
    all_to_all x1, waiting for transfers between devices, on_device(): lax.all_to_all(send_rows.reshape(ranks, cap, width), 'seq', split_axis=0,...  11.8 us
  transfers between devices with their start and end apart: 7, of which 6 were waited for; matrix products, arithmetic and copies ran while one was open for 14% of the time, Pallas kernels for 0%

commit v1 on v0

--- a/solution.py
+++ b/solution.py
@@ -10,6 +10,12 @@
 highest = lax.Precision.HIGHEST
 far_query = 536870912
 far_key = 1073741824
+
+
+def in_order(blocks, dim):
+    blocks = jnp.moveaxis(blocks, 0, dim)
+    shape = blocks.shape
+    return blocks.reshape(*shape[:dim], shape[dim] * shape[dim + 1], *shape[dim + 2 :])
 
 
 def carried_in(shard, axis, combine, identity):
@@ -217,7 +223,19 @@
         .reshape(slots, heads_main, HD)
     )
     key_pos_here = jnp.where(valid, got_pos, far_key)
-    key_rows = lax.all_gather(keys_here, "seq", axis=0, tiled=True)
+    devices = lax.axis_size("seq")
+    pairs = [(i, (i + 1) % devices) for i in range(devices)]
+    back = [(b_2, a_2) for a_2, b_2 in pairs]
+    lower, upper = ([], [])
+    for step in range(devices - 1):
+        if step % 2 == 0:
+            lower.append(lax.ppermute(lower[-1] if lower else keys_here, "seq", pairs))
+        else:
+            upper.append(lax.ppermute(upper[-1] if upper else keys_here, "seq", back))
+    blocks_2 = jnp.stack([*lower[::-1], keys_here, *upper])
+    shift = lax.axis_index("seq") - len(lower)
+    blocks_2 = blocks_2[(jnp.arange(devices) - shift) % devices]
+    key_rows = in_order(blocks_2, 0)
     count = key_rows.shape[0]
     size = math.gcd(count, 512)
     nblk = count // size

time: 321 us -> 301 us (0.938)
  waiting for transfers between devices: 143 us -> 103 us
  local copies, waits for them, and re-layouts: 43 us -> 51.6 us
  starting transfers between devices: 13.2 us -> 21.5 us
    all_gather x1, waiting for transfers between devices: 42.5 us -> 0.01 us  [on_device(): lax.all_gather(values_here, 'seq', axis=0, tiled=True)]
    all_gather x1 -> x0, waiting for transfers between devices: 19.5 us -> none  [on_device(): key_rows = lax.all_gather(keys_here, 'seq', axis=0, tiled=True)]
    ppermute x0 -> x7, waiting for transfers between devices: none -> 18.7 us  [the longest x4 12.7 us: on_device(): lower.append(lax.ppermute(lower[-1] if lower else keys_here, 'seq', pairs))]
    ppermute x0 -> x7, starting transfers between devices: none -> 8.34 us  [the longest x3 4.99 us: on_device(): upper.append(lax.ppermute(upper[-1] if upper else keys_here, 'seq', back))]
    unnamed x44 -> x51, local copies, waits for them, and re-layouts: 3.06 us -> 9.68 us
    gather x0 -> x2, local copies, waits for them, and re-layouts: none -> 3.63 us  [on_device(): blocks_2 = blocks_2[(jnp.arange(devices) - shift) % devices]]
  transfers between devices with their start and end apart: 7 -> 13, of which waited for: 6 -> 7; matrix products, arithmetic and copies ran while one was open for 14% -> 18% of each run, Pallas kernels for 0% -> 0%
where the time goes in v1:
time: 301 us; the launch traced here: 298 us
  waiting for transfers between devices  103 us (34%)
  local copies, waits for them, and re-layouts  51.6 us (17%)
  blocking collectives  42.3 us (14%)
  matrix products  34.6 us (11%)
  other arithmetic  30.7 us (10%)
  starting transfers between devices  21.5 us (7%)
  between operations  14.2 us (5%)
    psum x1, waiting for transfers between devices, on_device(): lax.psum(partial_enc.astype(jnp.bfloat16), 'tp').astype(jnp.float32)  34.8 us
    psum x1, waiting for transfers between devices, on_device(): lax.psum(jnp.dot(attended, w_o, preferred_element_type=jnp.float32).astyp...  34.8 us
    dynamic_update_slice x4, local copies, waits for them, and re-layouts, ssd_blocks(): final, outs = lax.scan(advance, start_state, blocks)  24.1 us
    all_gather x1, blocking collectives, carried_in(): lax.all_gather(part.astype(kind), axis)  21.2 us
    all_gather x1, blocking collectives, on_device(): lax.all_gather(shortened(key_pos_here), 'seq', axis=0, tiled=True)  21.1 us
    ppermute x4, waiting for transfers between devices, on_device(): lower.append(lax.ppermute(lower[-1] if lower else keys_here, 'seq', pairs))  12.7 us
    all_to_all x1, waiting for transfers between devices, on_device(): lax.all_to_all(send_rows.reshape(ranks, cap, width), 'seq', split_axis=0,...  11.8 us
    unnamed x51, local copies, waits for them, and re-layouts  9.68 us
  transfers between devices with their start and end apart: 13, of which 7 were waited for; matrix products, arithmetic and copies ran while one was open for 18% of the time, Pallas kernels for 0%

profile of v1, /device:TPU:0, one launch (start us, length us, event | category | flops | bytes accessed | tf_op | source)
XLA Modules:
  0.0 298.3 jit_solution(14633987886940390819)
XLA Ops:
  8.9 2.0 convolution_convert_fusion.4
  12.5 32.7 %while.42 = (s32[]{:T(128)}, f32[4,128,128]{2,1,0:T(8,128)S(1)}, f32[2,256,4,128]{1,0,3,2:T(2,128)}, f32[2,256,4]{1,2,0:T(4,128)S(1)}, bf16[2,256,128]{2,1,0:T(8...) while((s32[]{:T(128)}, f32[4,128,128]{2,1,0:T(8,128)S(1)}, ...), condition=%wide.region_4.5_spmd.clone, body=%wide.region_1.4_spmd.clone.sunk | while | flops 823755776 | bytes 7013988 | solution.py:89
  17.3 11.5 %dynamic_update_slice.6 = f32[2,256,4,128]{1,0,3,2:T(2,128)} dynamic-update-slice(f32[2,256,4,128]{1,0,3,2:T(2,128)} %get-tuple-element.594, f32[1,256,4,128]{1,0,3,2:T(1,128)S(1)} %copy.196, s32[]{:T(128)S(6)} %copy.201, s32[]{:T(128)} %constant.123.clone.1..sunk, s32[]{:T(128)} %constant.123.clone.1..sunk, s32[]{:T(128)} %constant.123.clone.1..sunk) | dynamic-update-slice | bytes 1048580 | tf_op jit(solution)/shard_map/while/body/jit(dynamic_update_index_in_dim)/dynamic_update_slice | solution.py:89
  33.7 11.5 %dynamic_update_slice.6 = f32[2,256,4,128]{1,0,3,2:T(2,128)} dynamic-update-slice(f32[2,256,4,128]{1,0,3,2:T(2,128)} %get-tuple-element.594, f32[1,256,4,128]{1,0,3,2:T(1,128)S(1)} %copy.196, s32[]{:T(128)S(6)} %copy.201, s32[]{:T(128)} %constant.123.clone.1..sunk, s32[]{:T(128)} %constant.123.clone.1..sunk, s32[]{:T(128)} %constant.123.clone.1..sunk) | dynamic-update-slice | bytes 1048580 | tf_op jit(solution)/shard_map/while/body/jit(dynamic_update_index_in_dim)/dynamic_update_slice | solution.py:89
  49.6 7.3 %all-to-all-start = ((s32[8,1,32]{2,1,0:T(1,128)}), s32[8,1,32]{2,1,0:T(1,128)}, u32[]{:S(2)}, u32[]{:S(2)}) async-start(s32[8,1,32]{2,1,0:T(1,128)} %select_n.96), calls=%async_computation | async-start | bytes 8192 | tf_op jit(solution)/shard_map/all_to_all | solution.py:192
  56.9 21.2 %all-gather.1 = bf16[8,1,4]{2,1,0:T(2,128)(2,1)} all-gather(bf16[1,1,4]{2,1,0:T(2,128)(2,1)S(1)} %slice_bitcast_fusion), channel_id=1, replica_groups=mesh['seq'=8,'tp'=4] {'seq'}, dimensions={0}, use_global_device_ids=true | all-gather | bytes 72 | tf_op jit(solution)/shard_map/all_gather | solution.py:24
  78.1 2.1 reshape.283
  83.3 3.2 %divide_multiply_fusion = f32[512,512]{0,1:T(8,128)} fusion(bf16[1024,512]{1,0:T(8,128)(2,1)} %param.24, bf16[512,1024]{1,0:T(8,128)(2,1)S(1)} %copy-done.5, f32[512]{0:T(512)} %copy-done.16), kind=kOutput, calls=%fused_computation.93 | convolution fusion | flops 539492352 | bytes 3147776 | tf_op jit(solution)/shard_map/dot_general | solution.py:137
  86.5 2.8 all-gather.8.cloned.1.call-done
  89.3 13.7 %while.43 = (s32[]{:T(128)}, f32[4,128,128]{2,1,0:T(8,128)S(1)}, s32[]{:T(128)}, bf16[8,4]{1,0:T(8,128)(2,1)}, bf16[8,4,128,128]{3,2,1,0:T(8,128)(2,1)}, /*index=5*/s32[]{:T(128)}, s32[]{:T(128)}) while((s32[]{:T(128)}, f32[4,128,128]{2,1,0:T(8,128)S(1)}, s32[]{:T(128)}, bf16[8,4]{1,0:T(8,128)(2,1)}, ...), condition=%wide.region_8.9_spmd.clone, body=%wide.region_7.8_spmd.clone.sunk | while | flops 327688 | bytes 655513 | solution.py:41
  109.2 34.8 %all-reduce.3.cloned.1.call-done = bf16[512,1024]{1,0:T(8,128)(2,1)} async-done(((bf16[512,1024]{1,0:T(8,128)(2,1)}), bf16[512,1024]{1,0:T(8,128)(2,1)}) %all-reduce.3.cloned.1.call-update) | async-done | bytes 1048592 | tf_op jit(solution)/shard_map/psum | solution.py:164
  146.9 5.5 %all-to-all-start.1 = ((bf16[8,32,1024]{2,1,0:T(8,128)(2,1)}), bf16[8,32,1024]{2,1,0:T(8,128)(2,1)S(1)}, u32[]{:S(2)}, u32[]{:S(2)}) async-start(bf16[8,32,1024]{2,1,0:T(8,128)(2,1)} %bitcast.199), calls=%async_computation.1 | async-start | bytes 1048576 | tf_op jit(solution)/shard_map/all_to_all | solution.py:189
  154.6 11.8 %all-to-all-done.1 = bf16[8,32,1024]{2,1,0:T(8,128)(2,1)S(1)} async-done(((bf16[8,32,1024]{2,1,0:T(8,128)(2,1)}), bf16[8,32,1024]{2,1,0:T(8,128)(2,1)S(1)}, u32[]{:S(2)}, u32[]{:S(2)}) %all-to-all-start.1) | async-done | bytes 524320 | tf_op jit(solution)/shard_map/all_to_all | solution.py:189
  173.1 7.0 %collective-permute-done = bf16[256,3,128]{0,2,1:T(8,128)(2,1)S(1)} collective-permute-done((bf16[256,3,128]{0,2,1:T(8,128)(2,1)S(1)}, bf16[256,3,128]{0,2,1:T(8,128)(2,1)S(1)}, u32[]{:S(2)}, u32[]{:S(2)}) %collective-permute-start) | collective-permute-done | bytes 196640 | tf_op jit(solution)/shard_map/ppermute | solution.py:232
  180.2 4.8 %collective-permute-start.4 = (bf16[256,3,128]{0,2,1:T(8,128)(2,1)S(1)}, bf16[256,3,128]{0,2,1:T(8,128)(2,1)S(1)}, u32[]{:S(2)}, u32[]{:S(2)}) collective-permute-start(bf16[256,3,128]{0,2,1:T(8,128)(2,1)S(1)} %bitcast.203), channel_id=1, source_target_pairs={{4,0},{8,4},{12,8},{16,12},{20,16},{24,20},{28,24},{0,28},{5,1},{9... | collective-permute-start | bytes 589832 | tf_op jit(solution)/shard_map/ppermute | solution.py:234
  185.0 5.6 %collective-permute-done.1 = bf16[256,3,128]{0,2,1:T(8,128)(2,1)S(1)} collective-permute-done((bf16[256,3,128]{0,2,1:T(8,128)(2,1)S(1)}, bf16[256,3,128]{0,2,1:T(8,128)(2,1)S(1)}, u32[]{:S(2)}, u32[]{:S(2)}) %collective-permute-start.1) | collective-permute-done | bytes 196640 | tf_op jit(solution)/shard_map/ppermute | solution.py:232
  190.6 21.1 %all-gather.2 = s32[8,1,256]{2,1,0:T(1,128)S(1)} all-gather(s32[1,1,256]{2,1,0:T(1,128)S(1)} %bitcast.220), channel_id=1, replica_groups=mesh['seq'=8,'tp'=4] {'seq'}, dimensions={0}, use_global_device_ids=true | all-gather | bytes 9216 | tf_op jit(solution)/shard_map/all_gather | solution.py:249
  213.9 2.6 convolution_convert_fusion.7
  217.7 6.0 %collective-permute-done.5 = bf16[256,3,128]{0,2,1:T(8,128)(2,1)} collective-permute-done((bf16[256,3,128]{0,2,1:T(8,128)(2,1)S(1)}, bf16[256,3,128]{0,2,1:T(8,128)(2,1)}, u32[]{:S(2)}, u32[]{:S(2)}) %collective-permute-start.5) | collective-permute-done | bytes 196640 | tf_op jit(solution)/shard_map/ppermute | solution.py:234
  231.0 2.1 gather_fusion
  234.7 2.6 copy.149
  237.3 14.2 %while.44 = (s32[]{:T(128)}, f32[3,256]{1,0:T(4,128)S(1)}, f32[3,256]{1,0:T(4,128)S(1)}, f32[256,3,128]{0,2,1:T(8,128)S(1)}, s32[4,512]{1,0:T(4,128)S(1)}, /*ind...) while((s32[]{:T(128)}, f32[3,256]{1,0:T(4,128)S(1)}, ...), condition=%wide.region_21.22_spmd.clone, body=%wide.region_18.21_spmd.clone.sunk | while | flops 205296128 | bytes 7068813 | solution.py:251
  254.7 34.8 %all-reduce.5.cloned.1.call-done = bf16[256,1536]{1,0:T(8,128)(2,1)} async-done(((bf16[256,1536]{1,0:T(8,128)(2,1)}), bf16[256,1536]{1,0:T(8,128)(2,1)}) %all-reduce.5.cloned.1.call-update) | async-done | bytes 786448 | tf_op jit(solution)/shard_map/psum | solution.py:257
  289.5 2.3 fusion.51
  (229 shorter events, 81.0 us)
Async XLA Ops:
  7.2 244.3 %copy-start = (bf16[384,1536]{1,0:T(8,128)(2,1)S(1)}, bf16[384,1536]{1,0:T(8,128)(2,1)}, u32[]{:S(2)}) copy-start(bf16[384,1536]{1,0:T(8,128)(2,1)} %param.31) | copy-start | bytes 3538948
  7.2 82.1 %all-gather.8.cloned.1.call-start = ((), (), s32[]{:S(2)}) async-start(), calls=%async_computation.5 | async-start | bytes 1179648 | tf_op jit(solution)/shard_map/all_gather | solution.py:24
  8.9 3.5 %copy-start.16 = (f32[512]{0:T(512)}, f32[512]{0:T(512)S(1)}, u32[]{:S(2)}) copy-start(f32[512]{0:T(512)S(1)} %add_rsqrt_fusion.1) | copy-start | bytes 6148
  12.5 35.3 %copy-start.13 = (s32[128,1]{0,1:T(1,128)S(1)}, s32[128,1]{0,1:T(1,128)}, u32[]{:S(2)}) copy-start(s32[128,1]{0,1:T(1,128)} %param.21) | copy-start | bytes 1540
  45.2 38.1 %copy-start.5 = (bf16[512,1024]{1,0:T(8,128)(2,1)S(1)}, bf16[512,1024]{1,0:T(8,128)(2,1)}, u32[]{:S(2)}) copy-start(bf16[512,1024]{1,0:T(8,128)(2,1)} %param.19) | copy-start | bytes 3145732
  49.6 97.4 %all-to-all-start = ((s32[8,1,32]{2,1,0:T(1,128)}), s32[8,1,32]{2,1,0:T(1,128)}, u32[]{:S(2)}, u32[]{:S(2)}) async-start(s32[8,1,32]{2,1,0:T(1,128)} %select_n.96), calls=%async_computation | async-start | bytes 8192 | tf_op jit(solution)/shard_map/all_to_all | solution.py:192
  56.9 87.1 %all-reduce.3.cloned.1.call-start = ((), (), s32[]{:S(2)}) async-start(), calls=%async_computation.2 | async-start | bytes 2097152 | tf_op jit(solution)/shard_map/psum | solution.py:164
  109.2 36.4 %copy-start.15 = (s32[128]{0:T(128)S(1)}, s32[128]{0:T(128)}, u32[]{:S(2)}) copy-start(s32[128]{0:T(128)} %copy-done.14) | copy-start | bytes 1540
  145.6 21.0 %copy-start.1 = (bf16[512,1024]{1,0:T(8,128)(2,1)}, bf16[512,1024]{1,0:T(8,128)(2,1)S(1)}, u32[]{:S(2)}) copy-start(bf16[512,1024]{1,0:T(8,128)(2,1)S(1)} %fusion.47) | copy-start | bytes 3145732
  145.6 8.8 %copy-start.17 = (bf16[512]{0:T(512)(128)(2,1)S(1)}, bf16[512]{0:T(512)(128)(2,1)}, u32[]{:S(2)}) copy-start(bf16[512]{0:T(512)(128)(2,1)} %param.27) | copy-start | bytes 3076
  146.9 19.5 %all-to-all-start.1 = ((bf16[8,32,1024]{2,1,0:T(8,128)(2,1)}), bf16[8,32,1024]{2,1,0:T(8,128)(2,1)S(1)}, u32[]{:S(2)}, u32[]{:S(2)}) async-start(bf16[8,32,1024]{2,1,0:T(8,128)(2,1)} %bitcast.199), calls=%async_computation.1 | async-start | bytes 1048576 | tf_op jit(solution)/shard_map/all_to_all | solution.py:189
  152.4 82.2 %all-gather.6.cloned.1.call-start = ((), (), s32[]{:S(2)}) async-start(), calls=%async_computation.3 | async-start | bytes 1769472 | tf_op jit(solution)/shard_map/all_gather | solution.py:248
  154.5 59.3 %copy-start.6 = (bf16[256,512]{1,0:T(8,128)(2,1)}, bf16[256,512]{1,0:T(8,128)(2,1)S(1)}, u32[]{:S(2)}) copy-start(bf16[256,512]{1,0:T(8,128)(2,1)S(1)} %broadcast_select_fusion) | copy-start | bytes 786436
  166.4 47.5 %copy-start.2 = (bf16[8,32,1024]{2,1,0:T(8,128)(2,1)}, bf16[8,32,1024]{2,1,0:T(8,128)(2,1)S(1)}, u32[]{:S(2)}) copy-start(bf16[8,32,1024]{2,1,0:T(8,128)(2,1)S(1)} %all-to-all-done.1) | copy-start | bytes 1572868
  169.4 120.1 %all-reduce.5.cloned.1.call-start = ((), (), s32[]{:S(2)}) async-start(), calls=%async_computation.4 | async-start | bytes 1572864 | tf_op jit(solution)/shard_map/psum | solution.py:257
  171.7 8.5 %collective-permute-start = (bf16[256,3,128]{0,2,1:T(8,128)(2,1)S(1)}, bf16[256,3,128]{0,2,1:T(8,128)(2,1)S(1)}, u32[]{:S(2)}, u32[]{:S(2)}) collective-permute-start(bf16[256,3,128]{0,2,1:T(8,128)(2,1)S(1)} %bitcast.202), channel_id=1, source_target_pairs={{0,4},{4,8},{8,12},{12,16},{16,20},{20,24},{24,28},{28,0},{1,5},{5... | collective-permute-start | bytes 589832 | tf_op jit(solution)/shard_map/ppermute | solution.py:232
  180.2 10.4 %collective-permute-start.1 = (bf16[256,3,128]{0,2,1:T(8,128)(2,1)S(1)}, bf16[256,3,128]{0,2,1:T(8,128)(2,1)S(1)}, u32[]{:S(2)}, u32[]{:S(2)}) collective-permute-start(bf16[256,3,128]{0,2,1:T(8,128)(2,1)S(1)} %collective-permute-done), channel_id=1, source_target_pairs={{0,4},{4,8},{8,12},{12,16},{16,20},{20,24},{24,28},{28,0},{1,5},{5... | collective-permute-start | bytes 589832 | tf_op jit(solution)/shard_map/ppermute | solution.py:232
  180.2 31.6 %collective-permute-start.4 = (bf16[256,3,128]{0,2,1:T(8,128)(2,1)S(1)}, bf16[256,3,128]{0,2,1:T(8,128)(2,1)S(1)}, u32[]{:S(2)}, u32[]{:S(2)}) collective-permute-start(bf16[256,3,128]{0,2,1:T(8,128)(2,1)S(1)} %bitcast.203), channel_id=1, source_target_pairs={{4,0},{8,4},{12,8},{16,12},{20,16},{24,20},{28,24},{0,28},{5,1},{9... | collective-permute-start | bytes 589832 | tf_op jit(solution)/shard_map/ppermute | solution.py:234
  190.6 21.4 %collective-permute-start.2 = (bf16[256,3,128]{0,2,1:T(8,128)(2,1)S(1)}, bf16[256,3,128]{0,2,1:T(8,128)(2,1)S(1)}, u32[]{:S(2)}, u32[]{:S(2)}) collective-permute-start(bf16[256,3,128]{0,2,1:T(8,128)(2,1)S(1)} %collective-permute-done.1), channel_id=1, source_target_pairs={{0,4},{4,8},{8,12},{12,16},{16,20},{20,24},{24,28},{28,0},{1,5},{5... | collective-permute-start | bytes 589832 | tf_op jit(solution)/shard_map/ppermute | solution.py:232
  211.8 11.9 %collective-permute-start.5 = (bf16[256,3,128]{0,2,1:T(8,128)(2,1)S(1)}, bf16[256,3,128]{0,2,1:T(8,128)(2,1)}, u32[]{:S(2)}, u32[]{:S(2)}) collective-permute-start(bf16[256,3,128]{0,2,1:T(8,128)(2,1)S(1)} %collective-permute-done.4), channel_id=1, source_target_pairs={{4,0},{8,4},{12,8},{16,12},{20,16},{24,20},{28,24},{0,28},{5,1},{9... | collective-permute-start | bytes 589832 | tf_op jit(solution)/shard_map/ppermute | solution.py:234
  212.0 11.7 %collective-permute-start.3 = (bf16[256,3,128]{0,2,1:T(8,128)(2,1)S(1)}, bf16[256,3,128]{0,2,1:T(8,128)(2,1)}, u32[]{:S(2)}, u32[]{:S(2)}) collective-permute-start(bf16[256,3,128]{0,2,1:T(8,128)(2,1)S(1)} %collective-permute-done.2), channel_id=1, source_target_pairs={{0,4},{4,8},{8,12},{12,16},{16,20},{20,24},{24,28},{28,0},{1,5},{5... | collective-permute-start | bytes 589832 | tf_op jit(solution)/shard_map/ppermute | solution.py:232
  223.7 6.7 %collective-permute-start.6 = (bf16[256,3,128]{0,2,1:T(8,128)(2,1)}, bf16[256,3,128]{0,2,1:T(8,128)(2,1)S(1)}, u32[]{:S(2)}, u32[]{:S(2)}) collective-permute-start(bf16[256,3,128]{0,2,1:T(8,128)(2,1)} %collective-permute-done.5), channel_id=1, source_target_pairs={{4,0},{8,4},{12,8},{16,12},{20,16},{24,20},{28,24},{0,28},{5,1},{9... | collective-permute-start | bytes 589832 | tf_op jit(solution)/shard_map/ppermute | solution.py:234
  251.5 38.0 %copy-start.3 = (bf16[8,32,1024]{2,1,0:T(8,128)(2,1)S(1)}, bf16[8,32,1024]{2,1,0:T(8,128)(2,1)}, u32[]{:S(2)}) copy-start(bf16[8,32,1024]{2,1,0:T(8,128)(2,1)} %copy-done.2) | copy-start | bytes 1572868
  251.5 38.0 %copy-start.7 = (bf16[256,512]{1,0:T(8,128)(2,1)S(1)}, bf16[256,512]{1,0:T(8,128)(2,1)}, u32[]{:S(2)}) copy-start(bf16[256,512]{1,0:T(8,128)(2,1)} %copy-done.6) | copy-start | bytes 786436
  (9 other events, 14.2 us)
Sparse Core Ops, SparseCore 0:
  46.1 43.2 all-gather.7
  109.1 34.8 all-reduce.2
  169.5 60.5 all-gather.5
  253.1 36.2 all-reduce.4
